TPU v7x, 256 devices: a whole 4x4x8 slice. The times are simulated.
256 devices in a mesh: row: 8 (over z_hi, core), col: 32 (over y, x, z_lo).
Axes of the slice: x: 4, y: 4, z: 8 (z_hi: 4, z_lo: 2; z = z_hi * 2 + z_lo), core: 2. Of those that a mesh axis runs over, the one named last changes fastest.
Arguments:
- tile_amps: bfloat16 [6144, 6144], P('row', 'col'), as said below
- cycle_ints: bfloat16 [6144, 6144], P('row', 'col'), as said below
- base_ints: bfloat16 [6144, 6144], P('row', 'col'), as said below
- amp_mask: int32 [96, 96], P('row', 'col'), may hold values from 0 to 1, as said below
- int_mask: int32 [96, 96], P('row', 'col'), may hold values from 0 to 1, as said below
- pair_amps: bfloat16 [64, 196608], P(None, ('row', 'col')), may hold values from -6 to 6
- ladder_ints: bfloat16 [196608, 1024], P(('row', 'col')), may hold values from -0.0546875 to 0.0546875
- pair_list: int32 [16], replicated, may hold values from 0 to 63, as said below
Outputs:
- cycle_residual: float32 [6144, 6144], P('row', 'col')
- ladder: float32 [16, 1024], P(None, 'col')
Inputs may be any that keep to these rules, and one draw needn't show every extreme that they name: `tile_amps`: equal to its transpose. `cycle_ints`: equal to its transpose. `base_ints`: equal to its transpose. `amp_mask`: 0 or 1, equal to its transpose, 1 on every diagonal tile. `int_mask`: 0 or 1, equal to its transpose, 1 on every diagonal tile. `pair_list`: distinct entries.
All inputs are finite; a program needn't handle non-finite values.
Results may differ from a plain program's by a relative error of at most 0.0029.
Values may be sent and summed in bfloat16 or wider, within the bound.
No kernel may reach another device: no remote copies, remote signals or barrier semaphores. Data moves between devices by JAX's collectives and lax.ppermute only.
A program may use at most 64 MiB of HBM per device.

v0:
```python
import jax
import jax.numpy as jnp
from jax import lax
from jax.sharding import PartitionSpec as P


def widen(mask, field):
    rows, cols = mask.shape
    tile = field.shape[0] // rows
    spread = jnp.broadcast_to(mask.astype(field.dtype)[:, None, :, None], (rows, tile, cols, tile))
    return field * spread.reshape(rows * tile, cols * tile)


def on_device(
    tile_amps, cycle_ints, base_ints, amp_mask, int_mask, pair_amps, ladder_ints, pair_list
):
    amplitudes = widen(amp_mask, tile_amps)
    integrals = widen(int_mask, cycle_ints)
    baseline = widen(int_mask, base_ints)
    amp_columns = lax.all_gather(amplitudes, "row", axis=0, tiled=True)
    section = amp_columns
    summed = baseline.astype(jnp.float32) + jnp.dot(
        lax.all_gather(integrals, "col", axis=1, tiled=True),
        section,
        preferred_element_type=jnp.float32,
    )
    intermediate = summed.astype(jnp.bfloat16)
    inter_columns = lax.all_gather(intermediate, "row", axis=0, tiled=True)
    section = inter_columns
    cycle_residual = jnp.dot(
        lax.all_gather(amplitudes, "col", axis=1, tiled=True),
        section,
        preferred_element_type=jnp.float32,
    )
    stored = pair_amps.shape[0]
    selector = (pair_list[:, None] == jnp.arange(stored, dtype=jnp.int32)[None, :]).astype(
        jnp.bfloat16
    )
    chosen = jnp.dot(selector, pair_amps, preferred_element_type=jnp.float32).astype(jnp.bfloat16)
    partial_sums = jnp.dot(chosen, ladder_ints, preferred_element_type=jnp.float32)
    totals = lax.psum(partial_sums, ("row", "col"))
    share_width = totals.shape[1] // lax.axis_size("col")
    ladder = lax.dynamic_slice_in_dim(totals, lax.axis_index("col") * share_width, share_width, 1)
    return (cycle_residual, ladder)


def solution(mesh):
    in_specs = (
        P("row", "col"),
        P("row", "col"),
        P("row", "col"),
        P("row", "col"),
        P("row", "col"),
        P(None, ("row", "col")),
        P(("row", "col"), None),
        P(),
    )
    out_specs = (P("row", "col"), P(None, "col"))
    return jax.shard_map(
        on_device, mesh=mesh, in_specs=in_specs, out_specs=out_specs, check_vma=False
    )
```

profile of v0, /device:TPU:1, one launch (start us, length us, event | category | flops | bytes accessed | tf_op | source)
XLA Modules:
  0.0 534.8 jit_solution(9945198933842615081)
XLA Ops:
  8.0 0.0 copy-start
  8.0 0.0 copy-start.3
  8.0 0.0 all-gather.9.cloned.1.call-start
  8.1 0.8 convert_element_type.17
  8.9 0.2 broadcast_in_dim.4
  9.0 0.5 reshape.14
  9.5 0.0 copy-start.2
  9.5 0.0 copy-start.4
  9.5 1.8 mul.12
  11.3 0.0 all-gather.9.cloned.1.call-update
  11.3 0.0 all-gather.7.cloned.1.call-start
  11.4 0.0 copy-done.3
  11.4 0.2 broadcast_in_dim.5
  11.6 0.0 copy-start.5
  11.6 0.5 reshape.15
  12.1 0.8 mul.14
  12.9 0.0 all-gather.7.cloned.1.call-update
  12.9 0.0 all-reduce.2.cloned.1.call-start
  13.0 1.1 fusion.1
  14.1 0.0 all-reduce.2.cloned.1.call-update
  14.1 0.0 all-gather.5.cloned.1.call-start
  14.2 0.7 all-gather.5.cloned.1.call-update
  14.9 0.0 all-gather.11.cloned.1.call-start
  14.9 39.0 %all-gather.9.cloned.1.call-done = bf16[6144,192]{0,1:T(8,128)(2,1)} async-done(((bf16[768,192]{0,1:T(8,128)(2,1)}), bf16[6144,192]{0,1:T(8,128)(2,1)}) %all-gather.9.cloned.1.call-update) | async-done | bytes 2359312 | tf_op jit(solution)/shard_map/all_gather | solution.py:20
  53.9 213.9 %all-gather.7.cloned.1.call-done = bf16[768,6144]{0,1:T(8,128)(2,1)} async-done(((bf16[768,192]{0,1:T(8,128)(2,1)}), bf16[768,6144]{0,1:T(8,128)(2,1)}) %all-gather.7.cloned.1.call-update) | async-done | bytes 9437200 | tf_op jit(solution)/shard_map/all_gather | solution.py:23
  267.8 7.1 %fusion = bf16[768,192]{0,1:T(8,128)(2,1)} fusion(bf16[6144,192]{0,1:T(8,128)(2,1)} %all-gather.9.cloned.1.call-done, bf16[768,6144]{0,1:T(8,128)(2,1)} %all-gather.7.cloned.1.call-done, bf16[768,192]{0,1:T(8,128)(2,1)S(1)} %copy-done.5, bf16[768,192]{0,1:T(8,128)(2,1)S(1)} %reshape.15), kind=kOutput, calls=%fused_computation.1 | convolution fusion | flops 1812529152 | bytes 12681216 | tf_op jit(solution)/shard_map/dot_general | solution.py:22
  274.9 0.0 all-gather.11.cloned.1.call-update
  275.0 101.3 %all-reduce.2.cloned.1.call-done = f32[16,1024]{1,0:T(8,128)} async-done(((f32[16,1024]{1,0:T(8,128)}), f32[16,1024]{1,0:T(8,128)}) %all-reduce.2.cloned.1.call-update) | async-done | bytes 65552 | tf_op jit(solution)/shard_map/psum | solution.py:41
  376.2 1.4 constant_dynamic-slice_fusion
  377.6 104.4 %all-gather.5.cloned.1.call-done = bf16[768,6144]{0,1:T(8,128)(2,1)} async-done(((bf16[768,192]{0,1:T(8,128)(2,1)}), bf16[768,6144]{0,1:T(8,128)(2,1)}) %all-gather.5.cloned.1.call-update) | async-done | bytes 9437200 | tf_op jit(solution)/shard_map/all_gather | solution.py:31
  482.0 38.5 %all-gather.11.cloned.1.call-done = bf16[6144,192]{0,1:T(8,128)(2,1)} async-done(((bf16[768,192]{0,1:T(8,128)(2,1)}), bf16[6144,192]{0,1:T(8,128)(2,1)}) %all-gather.11.cloned.1.call-update) | async-done | bytes 2359312 | tf_op jit(solution)/shard_map/all_gather | solution.py:28
  520.4 7.2 %fusion.4 = f32[768,192]{0,1:T(8,128)} fusion(bf16[6144,192]{0,1:T(8,128)(2,1)} %all-gather.11.cloned.1.call-done, bf16[768,6144]{0,1:T(8,128)(2,1)} %all-gather.5.cloned.1.call-done), kind=kOutput, calls=%fused_computation.7 | convolution fusion | flops 1811939328 | bytes 12386304 | tf_op jit(solution)/shard_map/dot_general | solution.py:30
  (7 shorter events, 0.0 us)
Async XLA Ops:
  8.0 5.0 copy-start
  8.0 3.4 copy-start.3
  8.0 45.9 %all-gather.9.cloned.1.call-start = ((), (), s32[]{:S(2)}) async-start(), calls=%async_computation.2 | async-start | bytes 2654208 | tf_op jit(solution)/shard_map/all_gather | solution.py:20
  8.9 3.2 copy-start.1
  9.5 3.5 copy-start.2
  9.5 3.5 copy-start.4
  11.3 256.5 %all-gather.7.cloned.1.call-start = ((), (), s32[]{:S(2)}) async-start(), calls=%async_computation.1 | async-start | bytes 9732096 | tf_op jit(solution)/shard_map/all_gather | solution.py:23
  11.6 256.2 %copy-start.5 = (bf16[768,192]{0,1:T(8,128)(2,1)S(1)}, bf16[768,192]{0,1:T(8,128)(2,1)}, u32[]{:S(2)}) copy-start(bf16[768,192]{0,1:T(8,128)(2,1)} %param.10) | copy-start | bytes 884740
  12.9 363.3 %all-reduce.2.cloned.1.call-start = ((), (), s32[]{:S(2)}) async-start(), calls=%async_computation.4 | async-start | bytes 131072 | tf_op jit(solution)/shard_map/psum | solution.py:41
  14.1 467.9 %all-gather.5.cloned.1.call-start = ((), (), s32[]{:S(2)}) async-start(), calls=%async_computation | async-start | bytes 9732096 | tf_op jit(solution)/shard_map/all_gather | solution.py:31
  14.9 505.6 %all-gather.11.cloned.1.call-start = ((), (), s32[]{:S(2)}) async-start(), calls=%async_computation.3 | async-start | bytes 2654208 | tf_op jit(solution)/shard_map/all_gather | solution.py:28
Sparse Core Ops, SparseCore 0:
  11.5 42.4 all-gather.8
  55.7 212.0 all-gather.6
  270.2 211.7 all-gather.4
  483.7 36.7 all-gather.10
Sparse Core Ops, SparseCore 1:
  18.9 357.3 all-reduce.1
where the time goes:
time: 535 us
  waiting for transfers between devices  498 us (93%)
  matrix products  15.4 us (3%)
  between operations  15.3 us (3%)
    all_gather x1, waiting for transfers between devices, on_device(): lax.all_gather(integrals, 'col', axis=1, tiled=True)  214 us
    all_gather x1, waiting for transfers between devices, on_device(): lax.all_gather(amplitudes, 'col', axis=1, tiled=True)  104 us
    psum x1, waiting for transfers between devices, on_device(): totals = lax.psum(partial_sums, ('row', 'col'))  101 us
    all_gather x1, waiting for transfers between devices, on_device(): amp_columns = lax.all_gather(amplitudes, 'row', axis=0, tiled=True)  39 us
    all_gather x1, waiting for transfers between devices, on_device(): inter_columns = lax.all_gather(intermediate, 'row', axis=0, tiled=True)  38.5 us
  transfers between devices with their start and end apart: 5, of which 5 were waited for; matrix products, arithmetic and copies ran while one was open for 2% of the time, Pallas kernels for 0%

commit v1 on v0

--- a/solution.py
+++ b/solution.py
@@ -38,7 +38,7 @@
     )
     chosen = jnp.dot(selector, pair_amps, preferred_element_type=jnp.float32).astype(jnp.bfloat16)
     partial_sums = jnp.dot(chosen, ladder_ints, preferred_element_type=jnp.float32)
-    totals = lax.psum(partial_sums, ("row", "col"))
+    totals = jnp.sum(lax.all_gather(partial_sums, ("row", "col")), axis=0)
     share_width = totals.shape[1] // lax.axis_size("col")
     ladder = lax.dynamic_slice_in_dim(totals, lax.axis_index("col") * share_width, share_width, 1)
     return (cycle_residual, ladder)

time: 535 us -> 1270 us (2.37)
  waiting for transfers between devices: 498 us -> 1220 us
    all_gather x0 -> x1, waiting for transfers between devices: none -> 724 us  [on_device(): totals = jnp.sum(lax.all_gather(partial_sums, ('row', 'col')), axis=0)]
    psum x1 -> x0, waiting for transfers between devices: 101 us -> none  [on_device(): totals = lax.psum(partial_sums, ('row', 'col'))]
    all_gather x1, waiting for transfers between devices: 104 us -> 206 us  [on_device(): lax.all_gather(amplitudes, 'col', axis=1, tiled=True)]
  transfers between devices with their start and end apart: 5 -> 5, of which waited for: 5 -> 5; matrix products, arithmetic and copies ran while one was open for 2% -> 1% of each run, Pallas kernels for 0% -> 0%
where the time goes in v1:
time: 1270 us; the launch traced here: 1260 us
  waiting for transfers between devices  1220 us (96%)
  matrix products  15.4 us (1%)
  between operations  13.9 us (1%)
    all_gather x1, waiting for transfers between devices, on_device(): totals = jnp.sum(lax.all_gather(partial_sums, ('row', 'col')), axis=0)  724 us
    all_gather x1, waiting for transfers between devices, on_device(): lax.all_gather(integrals, 'col', axis=1, tiled=True)  213 us
    all_gather x1, waiting for transfers between devices, on_device(): lax.all_gather(amplitudes, 'col', axis=1, tiled=True)  206 us
    all_gather x1, waiting for transfers between devices, on_device(): amp_columns = lax.all_gather(amplitudes, 'row', axis=0, tiled=True)  40.3 us
    all_gather x1, waiting for transfers between devices, on_device(): inter_columns = lax.all_gather(intermediate, 'row', axis=0, tiled=True)  37.9 us
  transfers between devices with their start and end apart: 5, of which 5 were waited for; matrix products, arithmetic and copies ran while one was open for 1% of the time, Pallas kernels for 0%

profile of v1, /device:TPU:1, one launch (start us, length us, event | category | flops | bytes accessed | tf_op | source)
XLA Modules:
  0.0 1263.3 jit_solution(3291934152193162963)
XLA Ops:
  7.2 0.0 copy-start
  7.2 0.0 all-gather.11.cloned.1.call-start
  7.2 0.8 convert_element_type.17
  8.0 0.2 broadcast_in_dim.4
  8.2 0.4 reshape.14
  8.6 0.0 copy-start.5
  8.7 1.8 mul.12
  10.4 0.0 all-gather.11.cloned.1.call-update
  10.5 0.0 all-gather.9.cloned.1.call-start
  10.5 0.2 broadcast_in_dim.5
  10.7 0.4 reshape.15
  11.2 0.8 mul.14
  11.9 0.0 all-gather.9.cloned.1.call-update
  12.0 0.0 all-gather.7.cloned.1.call-start
  12.0 0.7 all-gather.7.cloned.1.call-update
  12.7 0.0 copy-start.2
  12.7 0.0 copy-start.4
  12.7 0.0 all-gather.13.cloned.1.call-start
  12.8 40.3 %all-gather.11.cloned.1.call-done = bf16[6144,192]{0,1:T(8,128)(2,1)} async-done(((bf16[768,192]{0,1:T(8,128)(2,1)}), bf16[6144,192]{0,1:T(8,128)(2,1)}) %all-gather.11.cloned.1.call-update) | async-done | bytes 2359312 | tf_op jit(solution)/shard_map/all_gather | solution.py:20
  53.1 213.4 %all-gather.9.cloned.1.call-done = bf16[768,6144]{0,1:T(8,128)(2,1)} async-done(((bf16[768,192]{0,1:T(8,128)(2,1)}), bf16[768,6144]{0,1:T(8,128)(2,1)}) %all-gather.9.cloned.1.call-update) | async-done | bytes 9437200 | tf_op jit(solution)/shard_map/all_gather | solution.py:23
  266.4 7.1 fusion
  273.5 0.0 all-gather.13.cloned.1.call-update
  273.6 0.0 all-gather.15.cloned.1.call-start
  273.6 0.0 copy-done
  273.7 1.1 fusion.1
  274.7 0.0 all-gather.15.cloned.1.call-update
  274.8 205.5 %all-gather.7.cloned.1.call-done = bf16[768,6144]{0,1:T(8,128)(2,1)} async-done(((bf16[768,192]{0,1:T(8,128)(2,1)}), bf16[768,6144]{0,1:T(8,128)(2,1)}) %all-gather.7.cloned.1.call-update) | async-done | bytes 9437200 | tf_op jit(solution)/shard_map/all_gather | solution.py:31
  480.3 37.9 %all-gather.13.cloned.1.call-done = bf16[6144,192]{0,1:T(8,128)(2,1)} async-done(((bf16[768,192]{0,1:T(8,128)(2,1)}), bf16[6144,192]{0,1:T(8,128)(2,1)}) %all-gather.13.cloned.1.call-update) | async-done | bytes 2359312 | tf_op jit(solution)/shard_map/all_gather | solution.py:28
  518.2 7.2 fusion.4
  525.4 724.1 %all-gather.15.cloned.1.call-done = f32[4096,1024]{1,0:T(8,128)} async-done(((f32[16,1024]{1,0:T(8,128)}), f32[4096,1024]{1,0:T(8,128)}) %all-gather.15.cloned.1.call-update) | async-done | bytes 16777232 | tf_op jit(solution)/shard_map/all_gather | solution.py:41
  1249.5 6.6 reduce_sum.9
  1256.1 0.7 constant_dynamic-slice_fusion
  (8 shorter events, 0.0 us)
Async XLA Ops:
  7.2 266.5 %copy-start = (bf16[768,1024]{1,0:T(8,128)(2,1)S(1)}, bf16[768,1024]{1,0:T(8,128)(2,1)}, u32[]{:S(2)}) copy-start(bf16[768,1024]{1,0:T(8,128)(2,1)} %param.14) | copy-start | bytes 4718596
  7.2 3.3 copy-start.3
  7.2 45.9 %all-gather.11.cloned.1.call-start = ((), (), s32[]{:S(2)}) async-start(), calls=%async_computation.2 | async-start | bytes 2654208 | tf_op jit(solution)/shard_map/all_gather | solution.py:20
  8.0 3.1 copy-start.1
  8.6 257.8 %copy-start.5 = (bf16[768,192]{0,1:T(8,128)(2,1)S(1)}, bf16[768,192]{0,1:T(8,128)(2,1)}, u32[]{:S(2)}) copy-start(bf16[768,192]{0,1:T(8,128)(2,1)} %param.10) | copy-start | bytes 884740
  10.5 256.0 %all-gather.9.cloned.1.call-start = ((), (), s32[]{:S(2)}) async-start(), calls=%async_computation.1 | async-start | bytes 9732096 | tf_op jit(solution)/shard_map/all_gather | solution.py:23
  12.0 468.3 %all-gather.7.cloned.1.call-start = ((), (), s32[]{:S(2)}) async-start(), calls=%async_computation | async-start | bytes 9732096 | tf_op jit(solution)/shard_map/all_gather | solution.py:31
  12.7 260.9 %copy-start.2 = (bf16[64,768]{1,0:T(8,128)(2,1)S(1)}, bf16[64,768]{1,0:T(8,128)(2,1)}, u32[]{:S(2)}) copy-start(bf16[64,768]{1,0:T(8,128)(2,1)} %param.13) | copy-start | bytes 294916
  12.7 260.9 %copy-start.4 = (s32[16]{0:T(128)S(1)}, s32[16]{0:T(128)}, u32[]{:S(2)}) copy-start(s32[16]{0:T(128)} %param.15) | copy-start | bytes 196
  12.7 505.5 %all-gather.13.cloned.1.call-start = ((), (), s32[]{:S(2)}) async-start(), calls=%async_computation.3 | async-start | bytes 2654208 | tf_op jit(solution)/shard_map/all_gather | solution.py:28
  273.6 975.9 %all-gather.15.cloned.1.call-start = ((), (), s32[]{:S(2)}) async-start(), calls=%async_computation.4 | async-start | bytes 16842752 | tf_op jit(solution)/shard_map/all_gather | solution.py:41
Sparse Core Ops, SparseCore 0:
  10.6 42.4 all-gather.10
  54.9 211.5 all-gather.8
  268.8 211.4 all-gather.6
  482.0 36.1 all-gather.12
  519.9 729.5 all-gather.14

commit v2 on v0

--- a/solution.py
+++ b/solution.py
@@ -20,7 +20,9 @@
     amp_columns = lax.all_gather(amplitudes, "row", axis=0, tiled=True)
     section = amp_columns
     summed = baseline.astype(jnp.float32) + jnp.dot(
-        lax.all_gather(integrals, "col", axis=1, tiled=True),
+        jnp.concatenate(
+            lax.all_to_all(jnp.stack([integrals] * lax.axis_size("col")), "col", 0, 0), axis=1
+        ),
         section,
         preferred_element_type=jnp.float32,
     )

time: 535 us -> 511 us (0.955)
  waiting for transfers between devices: 498 us -> 461 us
  starting transfers between devices: 0.2 us -> 9.62 us
    all_gather x1 -> x0, waiting for transfers between devices: 214 us -> none  [on_device(): lax.all_gather(integrals, 'col', axis=1, tiled=True)]
    all_to_all x0 -> x1, waiting for transfers between devices: none -> 165 us  [on_device(): lax.all_to_all(jnp.stack([integrals] * lax.axis_size('col')), 'col', 0, 0)]
    psum x1, waiting for transfers between devices: 101 us -> 260 us  [on_device(): totals = lax.psum(partial_sums, ('row', 'col'))]
    all_gather x1, waiting for transfers between devices: 104 us -> 0.01 us  [on_device(): lax.all_gather(amplitudes, 'col', axis=1, tiled=True)]
    all_gather x1, waiting for transfers between devices: 38.5 us -> 0.01 us  [on_device(): inter_columns = lax.all_gather(intermediate, 'row', axis=0, tiled=True)]
    all_to_all x0 -> x1, starting transfers between devices: none -> 9.46 us  [on_device(): lax.all_to_all(jnp.stack([integrals] * lax.axis_size('col')), 'col', 0, 0)]
  transfers between devices with their start and end apart: 5 -> 5, of which waited for: 5 -> 3; matrix products, arithmetic and copies ran while one was open for 2% -> 3% of each run, Pallas kernels for 0% -> 0%
where the time goes in v2:
time: 511 us
  waiting for transfers between devices  461 us (90%)
  matrix products  15.6 us (3%)
  between operations  15.3 us (3%)
  starting transfers between devices  9.62 us (2%)
  local copies, waits for them, and re-layouts  7.37 us (1%)
    psum x1, waiting for transfers between devices, on_device(): totals = lax.psum(partial_sums, ('row', 'col'))  260 us
    all_to_all x1, waiting for transfers between devices, on_device(): lax.all_to_all(jnp.stack([integrals] * lax.axis_size('col')), 'col', 0, 0)  165 us
    all_gather x1, waiting for transfers between devices, on_device(): amp_columns = lax.all_gather(amplitudes, 'row', axis=0, tiled=True)  34.9 us
  transfers between devices with their start and end apart: 5, of which 3 were waited for; matrix products, arithmetic and copies ran while one was open for 3% of the time, Pallas kernels for 0%

profile of v2, /device:TPU:1, one launch (start us, length us, event | category | flops | bytes accessed | tf_op | source)
XLA Modules:
  0.0 511.2 jit_solution(16565238891689289322)
XLA Ops:
  8.0 0.0 copy-start
  8.0 0.0 copy-start.3
  8.0 0.0 all-gather.6.cloned.1.call-start
  8.1 0.8 convert_element_type.17
  8.9 0.2 broadcast_in_dim.4
  9.0 0.4 reshape.22
  9.5 1.7 mul.12
  11.2 0.0 all-gather.6.cloned.1.call-update
  11.2 0.0 copy-done.3
  11.3 0.2 broadcast_in_dim.5
  11.4 0.4 reshape.23
  11.9 0.0 copy-done.1
  11.9 0.1 mul.14
  12.0 4.8 stack.2
  16.8 9.5 %all-to-all-start = ((bf16[32,768,192]{1,2,0:T(8,128)(2,1)}), bf16[32,768,192]{1,2,0:T(8,128)(2,1)}, u32[]{:S(2)}, u32[]{:S(2)}) async-start(bf16[32,768,192]{1,2,0:T(8,128)(2,1)} %stack.2), calls=%async_computation | async-start | bytes 18874368 | tf_op jit(solution)/shard_map/all_to_all | solution.py:24
  26.2 0.0 all-reduce.2.cloned.1.call-start
  26.3 0.0 copy-done
  26.3 0.0 copy-done.2
  26.3 0.0 copy-done.4
  26.3 1.1 fusion.1
  27.4 0.0 all-reduce.2.cloned.1.call-update
  27.4 0.0 all-gather.4.cloned.1.call-start
  27.5 0.7 all-gather.4.cloned.1.call-update
  28.2 0.0 all-gather.8.cloned.1.call-start
  28.2 34.9 %all-gather.6.cloned.1.call-done = bf16[6144,192]{0,1:T(8,128)(2,1)} async-done(((bf16[768,192]{0,1:T(8,128)(2,1)}), bf16[6144,192]{0,1:T(8,128)(2,1)}) %all-gather.6.cloned.1.call-update) | async-done | bytes 2359312 | tf_op jit(solution)/shard_map/all_gather | solution.py:20
  63.1 165.2 %all-to-all-done = bf16[32,768,192]{1,2,0:T(8,128)(2,1)} async-done(((bf16[32,768,192]{1,2,0:T(8,128)(2,1)}), bf16[32,768,192]{1,2,0:T(8,128)(2,1)}, u32[]{:S(2)}, u32[]{:S(2)}) %all-to-all-start) | async-done | bytes 9437216 | tf_op jit(solution)/shard_map/all_to_all | solution.py:24
  228.2 0.0 copy-done.5
  228.2 7.3 %fusion = bf16[768,192]{0,1:T(8,128)(2,1)} fusion(bf16[6144,192]{0,1:T(8,128)(2,1)} %all-gather.6.cloned.1.call-done, bf16[768,6144]{0,1:T(8,128)(2,1)} %bitcast.1, bf16[768,192]{0,1:T(8,128)(2,1)S(1)} %copy-done.5, bf16[768,192]{0,1:T(8,128)(2,1)S(1)} %reshape.23), kind=kOutput, calls=%fused_computation.1 | convolution fusion | flops 1812529152 | bytes 12681216 | tf_op jit(solution)/shard_map/dot_general | solution.py:22
  235.5 0.0 all-gather.8.cloned.1.call-update
  235.6 259.9 %all-reduce.2.cloned.1.call-done = f32[16,1024]{1,0:T(8,128)} async-done(((f32[16,1024]{1,0:T(8,128)}), f32[16,1024]{1,0:T(8,128)}) %all-reduce.2.cloned.1.call-update) | async-done | bytes 65552 | tf_op jit(solution)/shard_map/psum | solution.py:43
  495.5 1.4 constant_dynamic-slice_fusion
  496.9 7.2 %fusion.4 = f32[768,192]{0,1:T(8,128)} fusion(bf16[6144,192]{0,1:T(8,128)(2,1)} %all-gather.8.cloned.1.call-done, bf16[768,6144]{0,1:T(8,128)(2,1)} %all-gather.4.cloned.1.call-done), kind=kOutput, calls=%fused_computation.7 | convolution fusion | flops 1811939328 | bytes 12386304 | tf_op jit(solution)/shard_map/dot_general | solution.py:32
  (7 shorter events, 0.0 us)
Async XLA Ops:
  8.0 18.3 %copy-start = (bf16[768,1024]{1,0:T(8,128)(2,1)S(1)}, bf16[768,1024]{1,0:T(8,128)(2,1)}, u32[]{:S(2)}) copy-start(bf16[768,1024]{1,0:T(8,128)(2,1)} %param.14) | copy-start | bytes 4718596
  8.0 3.2 copy-start.3
  8.0 55.0 %all-gather.6.cloned.1.call-start = ((), (), s32[]{:S(2)}) async-start(), calls=%async_computation.2 | async-start | bytes 2654208 | tf_op jit(solution)/shard_map/all_gather | solution.py:20
  8.9 3.0 copy-start.1
  16.7 9.5 %copy-start.2 = (bf16[64,768]{1,0:T(8,128)(2,1)S(1)}, bf16[64,768]{1,0:T(8,128)(2,1)}, u32[]{:S(2)}) copy-start(bf16[64,768]{1,0:T(8,128)(2,1)} %param.13) | copy-start | bytes 294916
  16.7 9.5 %copy-start.4 = (s32[16]{0:T(128)S(1)}, s32[16]{0:T(128)}, u32[]{:S(2)}) copy-start(s32[16]{0:T(128)} %param.15) | copy-start | bytes 196
  16.7 211.5 %copy-start.5 = (bf16[768,192]{0,1:T(8,128)(2,1)S(1)}, bf16[768,192]{0,1:T(8,128)(2,1)}, u32[]{:S(2)}) copy-start(bf16[768,192]{0,1:T(8,128)(2,1)} %param.10) | copy-start | bytes 884740
  16.8 211.5 %all-to-all-start = ((bf16[32,768,192]{1,2,0:T(8,128)(2,1)}), bf16[32,768,192]{1,2,0:T(8,128)(2,1)}, u32[]{:S(2)}, u32[]{:S(2)}) async-start(bf16[32,768,192]{1,2,0:T(8,128)(2,1)} %stack.2), calls=%async_computation | async-start | bytes 18874368 | tf_op jit(solution)/shard_map/all_to_all | solution.py:24
  26.2 469.3 %all-reduce.2.cloned.1.call-start = ((), (), s32[]{:S(2)}) async-start(), calls=%async_computation.4 | async-start | bytes 131072 | tf_op jit(solution)/shard_map/psum | solution.py:43
  27.4 469.5 %all-gather.4.cloned.1.call-start = ((), (), s32[]{:S(2)}) async-start(), calls=%async_computation.1 | async-start | bytes 9732096 | tf_op jit(solution)/shard_map/all_gather | solution.py:33
  28.2 468.7 %all-gather.8.cloned.1.call-start = ((), (), s32[]{:S(2)}) async-start(), calls=%async_computation.3 | async-start | bytes 2654208 | tf_op jit(solution)/shard_map/all_gather | solution.py:30
Sparse Core Ops, SparseCore 0:
  11.4 51.6 all-gather.5
  65.4 304.0 all-gather.3
  371.4 40.0 all-gather.7
Sparse Core Ops, SparseCore 1:
  32.2 463.2 all-reduce.1
